TPU v7x, 32 devices: a whole 2x2x4 slice. The times are simulated.
32 devices in a mesh: grp: 2 (over x), pan: 16 (over z, y, core).
Axes of the slice: x: 2, y: 2, z: 4, core: 2. Of those that a mesh axis runs over, the one named last changes fastest.
Arguments:
- pool_grads: bfloat16 [256, 8192], P(('grp', 'pan')), parts along dimension 0, may hold values from -6 to 6
- sample_idx: int32 [32, 4], P('grp'), parts along dimension 0, may hold values from 0 to 7
- basis: bfloat16 [16384, 8192], P('grp', 'pan'), parts along dimension 0, may hold values from -0.0625 to 0.0625
- rotations: bfloat16 [2, 2048, 8192], P(None, 'grp', 'pan'), parts along dimension 1, may hold values from -0.1875 to 0.1875
- jacobi_bits: int32 [8], P('grp'), parts along dimension 0, may hold values from 0 to 3, each once
Outputs:
- projected: bfloat16 [128, 8192], P('grp', 'pan'), parts along dimension 0
- scalings: float32 [16384], P(('grp', 'pan')), parts along dimension 0
- new_basis: bfloat16 [16384, 8192], P('grp', 'pan'), parts along dimension 0
There are 2 independent parts, one for each index of `grp`. A program takes and returns all parts, laid end to end along the dimension named above; each array names one. Nothing has to cross between parts.
Inputs may be any that keep to these rules, and one draw needn't show every extreme that they name: `jacobi_bits`: each of the 4 bits appears once.
All inputs are finite; a program needn't handle non-finite values.
Results may differ from a plain program's by a relative error of at most 0.0057.
Values may be sent and summed in bfloat16 or wider, within the bound.
No kernel may reach another device: no remote copies, remote signals or barrier semaphores. Data moves between devices by JAX's collectives and lax.ppermute only.
A program may use at most 128 MiB of HBM per device.

v0:
```python
from functools import partial

import jax
import jax.numpy as jnp
from jax import lax
from jax.sharding import PartitionSpec as P


def as_sent(x):
    return jax.tree.map(lambda a: a.astype(jnp.bfloat16) if a.dtype == jnp.float32 else a, x)


def swapped(x, axis, bit):
    return lax.ppermute(x, axis, [(i, i ^ 1 << bit) for i in range(lax.axis_size(axis))])


def swap_partner(panel_data, bit_number):
    return jax.tree.map(
        lambda part, own: part.astype(own.dtype),
        swapped(as_sent(panel_data), "pan", bit_number),
        panel_data,
    )


def body(pool_grads, sample_idx, basis, rotations, jacobi_bits):
    group_size = lax.axis_size("pan")
    bit_count = group_size.bit_length() - 1
    rows_here = pool_grads.shape[0]
    width = basis.shape[1]
    gathered = lax.all_gather(pool_grads, "pan", axis=0, tiled=True)
    offsets = jnp.arange(group_size, dtype=jnp.int32)[:, None] * rows_here
    flat_idx = (offsets + sample_idx).reshape(-1)
    samples = jnp.take(gathered, flat_idx, axis=0)
    branches = [partial(swap_partner, bit_number=bit_number) for bit_number in range(bit_count)]
    current = basis
    for step in range(rotations.shape[0]):
        other = lax.switch(jacobi_bits[step], branches, current)
        fresh = jnp.dot(current, rotations[step, :width], preferred_element_type=jnp.float32)
        fresh = fresh + jnp.dot(other, rotations[step, width:], preferred_element_type=jnp.float32)
        current = fresh.astype(jnp.bfloat16)
    full = jnp.dot(samples, current, preferred_element_type=jnp.float32)
    return (full.astype(jnp.bfloat16), jnp.mean(full * full, axis=0), current)


def solution(mesh):
    in_specs = (
        P(("grp", "pan"), None),
        P("grp", None),
        P("grp", "pan"),
        P(None, "grp", "pan"),
        P("grp"),
    )
    out_specs = (P("grp", "pan"), P(("grp", "pan")), P("grp", "pan"))
    return jax.shard_map(body, mesh=mesh, in_specs=in_specs, out_specs=out_specs, check_vma=False)
```

profile of v0, /device:TPU:0, one launch (start us, length us, event | category | flops | bytes accessed | tf_op | source)
XLA Modules:
  0.0 630.2 jit_solution(16245656330243156331)
XLA Ops:
  7.2 0.0 all-gather.2.cloned.1.call-start
  7.2 0.7 all-gather.2.cloned.1.call-update
  7.9 0.7 broadcast_add_fusion
  8.6 0.1 copy.10
  8.7 0.1 reshape.57
  8.8 0.1 reshape.56
  8.9 1.3 fusion.16
  10.8 368.9 %conditional.2 = (bf16[8192,512]{1,0:T(8,128)(2,1)}) conditional(s32[]{:T(128)} %bitcast.2, bf16[8192,512]{1,0:T(8,128)(2,1)} %param.15, bf16[8192,512]{1,0:T(8,128)(2,1)} %param.15, bf16[8192,512]{1,0:T(8,128)(2,1)} %param.15, bf16[8192,512]{1,0:T(8,128)(2,1)} %param.15), branch_computations={%region_0.1_spmd, %region_1.2_spmd, %region_2.3_spmd, %region_3.4_... | conditional | bytes 33554480 | solution.py:37
  10.9 4.1 collective-permute-start.3
  15.0 364.8 %collective-permute-done.3 = bf16[8192,512]{1,0:T(8,128)(2,1)} collective-permute-done((bf16[8192,512]{1,0:T(8,128)(2,1)}, bf16[8192,512]{1,0:T(8,128)(2,1)}, u32[]{:S(2)}, u32[]{:S(2)}) %collective-permute-start.3) | collective-permute-done | bytes 8388640 | tf_op jit(solution)/shard_map/cond/branch_3_fun/ppermute | solution.py:14
  379.8 0.0 copy-start
  379.8 13.8 %fusion.7 = f32[8192,512]{1,0:T(8,128)} fusion(bf16[8192,512]{1,0:T(8,128)(2,1)} %param.15, bf16[2,1024,512]{2,1,0:T(8,128)(2,1)} %param.16), kind=kOutput, calls=%fused_computation.10 | convolution fusion | flops 4294967296 | bytes 25690112 | tf_op jit(solution)/shard_map/dot_general | solution.py:38
  394.3 0.0 copy-done
  394.3 12.7 %add_convert_fusion.1 = bf16[8192,512]{1,0:T(8,128)(2,1)} fusion(f32[8192,512]{1,0:T(8,128)} %fusion.7, bf16[8192,512]{1,0:T(8,128)(2,1)} %get-tuple-element.26, bf16[2,1024,512]{2,1,0:T(8,128)(2,1)S(1)} %copy-done), kind=kOutput, calls=%fused_computation.2 | convolution fusion | flops 4303355904 | bytes 34078720 | tf_op jit(solution)/shard_map/dot_general | solution.py:39
  407.0 181.9 %conditional.3 = (bf16[8192,512]{1,0:T(8,128)(2,1)}) conditional(s32[]{:T(128)} %bitcast.5, bf16[8192,512]{1,0:T(8,128)(2,1)} %add_convert_fusion.1, bf16[8192,512]{1,0:T(8,128)(2,1)} %add_convert_fusion.1, bf16[8192,512]{1,0:T(8,128)(2,1)} %add_convert_fusion.1, bf16[8192,512]{1,0:T(8,128)(2,1)} %add_convert_fusion.1), branch_computations={%region_4.5_spmd, %region_5.6_spmd, %region_6.7_spmd, %region_7.8_... | conditional | bytes 33554480 | solution.py:37
  407.0 0.7 collective-permute-start.6
  407.7 181.2 %collective-permute-done.6 = bf16[8192,512]{1,0:T(8,128)(2,1)} collective-permute-done((bf16[8192,512]{1,0:T(8,128)(2,1)}, bf16[8192,512]{1,0:T(8,128)(2,1)}, u32[]{:S(2)}, u32[]{:S(2)}) %collective-permute-start.6) | collective-permute-done | bytes 8388640 | tf_op jit(solution)/shard_map/cond/branch_2_fun/ppermute | solution.py:14
  589.0 11.6 %fusion.4 = f32[8192,512]{1,0:T(8,128)} fusion(bf16[8192,512]{1,0:T(8,128)(2,1)} %add_convert_fusion.1, bf16[2,1024,512]{2,1,0:T(8,128)(2,1)S(1)} %copy-done), kind=kOutput, calls=%fused_computation.7 | convolution fusion | flops 4294967296 | bytes 25690112 | tf_op jit(solution)/shard_map/dot_general | solution.py:38
  600.6 12.5 %add_convert_fusion = bf16[8192,512]{1,0:T(8,128)(2,1)} fusion(f32[8192,512]{1,0:T(8,128)} %fusion.4, bf16[8192,512]{1,0:T(8,128)(2,1)} %get-tuple-element.27, bf16[2,1024,512]{2,1,0:T(8,128)(2,1)S(1)} %copy-done), kind=kOutput, calls=%fused_computation.1 | convolution fusion | flops 4303355904 | bytes 34078720 | tf_op jit(solution)/shard_map/dot_general | solution.py:39
  613.1 0.0 all-gather.2.cloned.1.call-done
  613.1 4.0 gather_fusion
  617.2 5.6 multiply_reduce_fusion
  622.8 0.6 broadcast_multiply_fusion
  (4 shorter events, 0.0 us)
Async XLA Ops:
  7.2 606.0 %all-gather.2.cloned.1.call-start = ((), (), s32[]{:S(2)}) async-start(), calls=%async_computation | async-start | bytes 2228224 | tf_op jit(solution)/shard_map/all_gather | solution.py:30
  10.9 368.9 %collective-permute-start.3 = (bf16[8192,512]{1,0:T(8,128)(2,1)}, bf16[8192,512]{1,0:T(8,128)(2,1)}, u32[]{:S(2)}, u32[]{:S(2)}) collective-permute-start(bf16[8192,512]{1,0:T(8,128)(2,1)} %param.3), channel_id=1, source_target_pairs={{0,8},{1,9},{2,10},{3,11},{4,12},{5,13},{6,14},{7,15},{8,0},{9,1},... | collective-permute-start | bytes 25165832 | tf_op jit(solution)/shard_map/cond/branch_3_fun/ppermute | solution.py:14
  379.8 14.5 %copy-start = (bf16[2,1024,512]{2,1,0:T(8,128)(2,1)S(1)}, bf16[2,1024,512]{2,1,0:T(8,128)(2,1)}, u32[]{:S(2)}) copy-start(bf16[2,1024,512]{2,1,0:T(8,128)(2,1)} %param.16) | copy-start | bytes 6291460
  407.0 181.9 %collective-permute-start.6 = (bf16[8192,512]{1,0:T(8,128)(2,1)}, bf16[8192,512]{1,0:T(8,128)(2,1)}, u32[]{:S(2)}, u32[]{:S(2)}) collective-permute-start(bf16[8192,512]{1,0:T(8,128)(2,1)} %param.6), channel_id=1, source_target_pairs={{0,4},{1,5},{2,6},{3,7},{4,0},{5,1},{6,2},{7,3},{8,12},{9,13},{10,... | collective-permute-start | bytes 25165832 | tf_op jit(solution)/shard_map/cond/branch_2_fun/ppermute | solution.py:14
Sparse Core Ops, SparseCore 0:
  10.2 392.9 all-gather.1
where the time goes:
time: 630 us
  waiting for transfers between devices  547 us (87%)
  matrix products  56.4 us (9%)
  between operations  15.4 us (2%)
    ppermute x2, waiting for transfers between devices, swapped(): lax.ppermute(x, axis, [(i, i ^ 1 << bit) for i in range(lax.axis_size(axi...  546 us
    dot_general x2, matrix products, body(): jnp.dot(current, rotations[step, :width], preferred_element_type=jnp.floa...  25.5 us
    dot_general x2, matrix products, body(): jnp.dot(other, rotations[step, width:], preferred_element_type=jnp.float32)  25.3 us
  transfers between devices with their start and end apart: 3, of which 2 were waited for; matrix products, arithmetic and copies ran while one was open for 8% of the time, Pallas kernels for 0%

commit v1 on v0

v1 whole, which is shorter than its diff:
```python
from functools import partial

import jax
import jax.numpy as jnp
from jax import lax
from jax.experimental import pallas as pl
from jax.experimental.pallas import tpu as pltpu
from jax.sharding import PartitionSpec as P

UNITS = 16
TILE = 128
HBM = pl.BlockSpec(memory_space=pltpu.HBM)


def plan(bits, width):
    if width < 256:
        return [8, 8]
    near = {0: 0, 1: 2, 2: 2}
    first, second = near.get(bits[0], 4), near.get(bits[1], 4)
    if 0 in (first, second):
        sizes = [2, 4, 5, 5]
    elif first != second:
        sizes = [1, 2, 3, 3, 3, 4]
    else:
        return [2] * 8
    return sizes if first < second else sizes[::-1]


def swapped(x, bit):
    return lax.ppermute(x, "pan", [(i, i ^ 1 << bit) for i in range(lax.axis_size("pan"))])


def after(x, *earlier):
    return lax.optimization_barrier((x, *earlier))[0]


def in_device_order(values, picked):
    me, count = lax.axis_index("pan"), lax.axis_size("pan")
    order = [0]
    for bit in reversed(range(count.bit_length() - 1)):
        order += [held ^ 1 << bit for held in order]
    source = jnp.array(order, jnp.int32) ^ me
    rows = (source[:, None] * picked + jnp.arange(picked, dtype=jnp.int32)).reshape(-1)
    pick = (jnp.arange(values.shape[0], dtype=jnp.int32)[:, None] == rows[None, :]).astype(values.dtype)
    return jnp.dot(pick, values, preferred_element_type=jnp.float32).astype(values.dtype)


def cost(rows, width, columns):
    return pl.CostEstimate(
        flops=2 * rows * width * columns, bytes_accessed=2 * (rows * width + width * columns + rows * columns), transcendentals=0
    )


def rotate(own, own_start, other, rotations, step, whole=None, start=0, depth=None):
    rows, width = other.shape
    tiles = rows // TILE

    def kernel(own_ref, other_ref, maps_ref, *rest):
        fresh_ref, own_held, other_held, map_held, fresh_held, map_sem, in_sems, out_sem = rest[-8:]

        def arrivals(i):
            at = pl.ds(pl.multiple_of(i * TILE, TILE), TILE)
            source = pl.ds(pl.multiple_of(own_start + i * TILE, TILE), TILE)
            return [
                pltpu.make_async_copy(own_ref.at[source], own_held.at[at], in_sems.at[0, i]),
                pltpu.make_async_copy(other_ref.at[at], other_held.at[at], in_sems.at[1, i]),
            ]

        def fetch(i, carry):
            for copy in arrivals(i):
                copy.start()
            return carry

        def tile(i, carry):
            for copy in arrivals(i):
                copy.wait()
            at = pl.ds(pl.multiple_of(i * TILE, TILE), TILE)
            target = pl.ds(pl.multiple_of(start + i * TILE, TILE), TILE)
            pair = jnp.concatenate([own_held[at], other_held[at]], axis=1)
            fresh = jnp.dot(pair, map_held[...], preferred_element_type=jnp.float32)
            fresh_held[at] = fresh.astype(jnp.bfloat16)
            pltpu.make_async_copy(fresh_held.at[at], fresh_ref.at[target], out_sem).start()
            return carry

        map_copy = pltpu.make_async_copy(maps_ref.at[step], map_held, map_sem)
        map_copy.start()
        lax.fori_loop(0, tiles, fetch, 0)
        map_copy.wait()
        lax.fori_loop(0, tiles, tile, 0)
        pltpu.make_async_copy(fresh_held, fresh_ref.at[pl.ds(start, rows)], out_sem).wait()

    args = [own, other, rotations] + [whole] * (whole is not None)
    return pl.pallas_call(
        kernel,
        in_specs=[HBM] * len(args),
        out_specs=HBM,
        out_shape=jax.ShapeDtypeStruct((depth or rows, width), jnp.bfloat16),
        scratch_shapes=[
            pltpu.VMEM((rows, width), jnp.bfloat16),
            pltpu.VMEM((rows, width), jnp.bfloat16),
            pltpu.VMEM((2 * width, width), jnp.bfloat16),
            pltpu.VMEM((rows, width), jnp.bfloat16),
            pltpu.SemaphoreType.DMA,
            pltpu.SemaphoreType.DMA((2, tiles)),
            pltpu.SemaphoreType.DMA,
        ],
        input_output_aliases={} if whole is None else {3: 0},
        compiler_params=pltpu.CompilerParams(vmem_limit_bytes=60 << 20),
        cost_estimate=cost(rows, 2 * width, width),
    )(*args)


def project(samples, basis, start, rows, full=None):
    width = basis.shape[1]
    count = samples.shape[0]
    tile = depth_tile(start, rows)
    first = start // tile

    def kernel(samples_ref, basis_ref, *rest):
        sum_ref = rest[-1]

        @pl.when(pl.program_id(0) == 0)
        def _():
            sum_ref[...] = jnp.zeros_like(sum_ref) if full is None else rest[0][...]

        sum_ref[...] += jnp.dot(samples_ref[...], basis_ref[...], preferred_element_type=jnp.float32)

    held = pl.BlockSpec((count, width), lambda i: (0, 0))
    return pl.pallas_call(
        kernel,
        grid=(rows // tile,),
        in_specs=[
            pl.BlockSpec((count, tile), lambda i: (0, first + i)),
            pl.BlockSpec((tile, width), lambda i: (first + i, 0)),
        ]
        + [held] * (full is not None),
        out_specs=held,
        out_shape=jax.ShapeDtypeStruct((count, width), jnp.float32),
        compiler_params=pltpu.CompilerParams(vmem_limit_bytes=60 << 20),
        cost_estimate=cost(count, rows, width),
    )(*([samples, basis] + [full] * (full is not None)))


def depth_tile(start, rows):
    tile = 512
    while start % tile or rows % tile:
        tile //= 2
    return tile


def joined(upper, lower):
    count = upper.shape[0]

    def kernel(upper_ref, lower_ref, whole_ref, sems):
        copies = [
            pltpu.make_async_copy(upper_ref, whole_ref.at[:count], sems.at[0]),
            pltpu.make_async_copy(lower_ref, whole_ref.at[count:], sems.at[1]),
        ]
        for copy in copies:
            copy.start()
        for copy in copies:
            copy.wait()

    return pl.pallas_call(
        kernel,
        in_specs=[HBM, HBM],
        out_specs=HBM,
        out_shape=jax.ShapeDtypeStruct((2 * count, *upper.shape[1:]), upper.dtype),
        scratch_shapes=[pltpu.SemaphoreType.DMA((2,))],
        compiler_params=pltpu.CompilerParams(vmem_limit_bytes=60 << 20),
        cost_estimate=pl.CostEstimate(flops=0, bytes_accessed=8 * upper.size, transcendentals=0),
    )(upper, lower)


def refresh(own, basis, rotations, bits):
    depth, width = basis.shape
    sizes = [units * depth // UNITS for units in plan(bits, width)]
    starts = [sum(sizes[:i]) for i in range(len(sizes))]
    chunks = len(sizes)
    picked, columns = own.shape
    gather_bits = list(reversed(range(lax.axis_size("pan").bit_length() - 1)))

    def send(chunk, *earlier):
        return swapped(after(basis, *earlier)[starts[chunk] : starts[chunk] + sizes[chunk]], bits[0])

    join_stages = [min(2 * i, chunks - 1) for i in range(1, len(gather_bits))]
    samples = own[None]
    sent = swapped(samples, gather_bits.pop(0))
    arriving = [send(0)]
    samples = joined(samples, sent)
    sent = swapped(samples, gather_bits.pop(0))
    arriving.append(send(1, samples))
    basis_out = middle = other = full = None
    for chunk in range(chunks):
        held = basis
        while join_stages and join_stages[0] == chunk and gather_bits:
            join_stages.pop(0)
            samples = joined(samples, sent)
            sent = swapped(samples, gather_bits.pop(0))
            held = after(basis, samples)
        fresh = rotate(held, starts[chunk], arriving[chunk], rotations, 0)
        coming = swapped(fresh, bits[1])
        if chunk + 2 < chunks:
            arriving.append(send(chunk + 2, fresh))
        if chunk > 0:
            basis_out = rotate(after(middle, fresh), 0, other, rotations, 1, basis_out, starts[chunk - 1], depth)
            if chunk + 1 < chunks:
                arriving[chunk + 1] = after(arriving[chunk + 1], basis_out)
        middle, other = fresh, coming
    while sent is not None:
        samples = joined(samples, sent)
        sent = swapped(samples, gather_bits.pop(0)) if gather_bits else None
    samples = samples.reshape(-1, columns)
    full = project(samples, basis_out, 0, starts[-1])
    basis_out = rotate(after(middle, full), 0, other, rotations, 1, basis_out, starts[-1], depth)
    full = project(samples, basis_out, starts[-1], sizes[-1], full)
    return full, basis_out


def body(pool_grads, sample_idx, basis, rotations, jacobi_bits):
    bit_count = lax.axis_size("pan").bit_length() - 1
    own = jnp.take(pool_grads, sample_idx[lax.axis_index("pan")], axis=0)
    pairs = [(a, b) for a in range(bit_count) for b in range(bit_count) if a != b]
    first, second = jacobi_bits[0], jacobi_bits[1]
    branch = first * (bit_count - 1) + second - (second > first).astype(jnp.int32)
    full, current = lax.switch(branch, [partial(refresh, bits=pair) for pair in pairs], own, basis, rotations)
    projected = in_device_order(full.astype(jnp.bfloat16), own.shape[0])
    return (projected, jnp.mean(full * full, axis=0), current)


def solution(mesh):
    in_specs = (
        P(("grp", "pan"), None),
        P("grp", None),
        P("grp", "pan"),
        P(None, "grp", "pan"),
        P("grp"),
    )
    out_specs = (P("grp", "pan"), P(("grp", "pan")), P("grp", "pan"))
    return jax.shard_map(body, mesh=mesh, in_specs=in_specs, out_specs=out_specs, check_vma=False)
```

time: 630 us -> 535 us (0.85)
  the two profiles are of different devices: /device:TPU:0 before, /device:TPU:2 now
where the time goes in v1:
time: 535 us; the launch traced here: 534 us
  waiting for transfers between devices  313 us (59%)
  Pallas kernels  137 us (26%)
  starting transfers between devices  29.6 us (6%)
  local copies, waits for them, and re-layouts  24.4 us (5%)
  loops' own time  23.9 us (4%)
    ppermute x16, waiting for transfers between devices, swapped(): lax.ppermute(x, 'pan', [(i, i ^ 1 << bit) for i in range(lax.axis_size('p...  313 us
    pallas_call x12, Pallas kernels, rotate(): pl.pallas_call(kernel, in_specs=[HBM] * len(args), out_specs=HBM, out_sha...  62.6 us
    pallas_call x4, Pallas kernels, joined(): pl.pallas_call(kernel, in_specs=[HBM, HBM], out_specs=HBM, out_shape=jax....  62 us
    ppermute x16, starting transfers between devices, swapped(): lax.ppermute(x, 'pan', [(i, i ^ 1 << bit) for i in range(lax.axis_size('p...  29.6 us
    another operation x1, loops' own time, body(): lax.switch(branch, [partial(refresh, bits=pair) for pair in pairs], own,...  23.9 us
    slice x6, local copies, waits for them, and re-layouts, send(): after(basis, *earlier)[starts[chunk]:starts[chunk] + sizes[chunk]]  15.3 us
    pallas_call x2, Pallas kernels, project(): pl.pallas_call(kernel, grid=(rows // tile,), in_specs=[pl.BlockSpec((coun...  12.4 us
  transfers between devices with their start and end apart: 16, of which 7 were waited for; matrix products, arithmetic and copies ran while one was open for 3% of the time, Pallas kernels for 25%

profile of v1, /device:TPU:2, one launch (start us, length us, event | category | flops | bytes accessed | tf_op | source)
XLA Modules:
  0.0 533.7 jit_solution(12617339859074802837)
XLA Ops:
  6.2 524.6 %conditional.1 = (f32[64,512]{1,0:T(8,128)S(1)}, bf16[8192,512]{1,0:T(8,128)(2,1)}) conditional(s32[]{:T(128)} %clamp.3, (bf16[4,8192]{1,0:T(4,128)(2,1)S(1)}, bf16[8192,512]{1,0:T(8,128)(2,1)}, bf16[2,1024,512]{2,1,0:T(8,128)(2,1)}) %tuple.236, (bf16[4,8192]{1,0:T(4,128)(2,1)S(1)}, bf16[8192,512]{1,0:T(8,128)(2,1)}, ...), branch_computations={%region_0.1_spmd, %region_1.2_spmd, %region_2.3_spmd, %region_3.4_... | conditional | flops 17716740096 | bytes 205390960 | solution.py:226
  29.6 3.0 slice.213
  35.6 93.3 %collective-permute-done.160.lower_ref = bf16[1,4,8192]{2,1,0:T(4,128)(2,1)S(1)} collective-permute-done((bf16[1,4,8192]{2,1,0:T(4,128)(2,1)S(1)}, bf16[1,4,8192]{2,1,0:T(4,128)(2,1)S(1)}, u32[]{:S(2)}, u32[]{:S(2)}) %collective-permute-start.160) | collective-permute-done | bytes 65568 | tf_op jit(solution)/shard_map/cond/branch_11_fun/ppermute | solution.py:30
  129.5 3.1 branch_11_fun.18.upper_ref
  132.6 2.7 slice.190
  135.3 7.0 %branch_11_fun.23.own_ref = bf16[2048,512]{1,0:T(8,128)(2,1)} custom-call(bf16[8192,512]{1,0:T(8,128)(2,1)} %get-tuple-element.281.own_ref, bf16[2048,512]{1,0:T(8,128)(2,1)} %collective-permute-done.166.other_ref, bf16[2,1024,512]{2,1,0:T(8,128)(2,1)S(1)} %copy-done.13), custom_call_target="tpu_custom_call" | custom-call | flops 2147483648 | bytes 7340032 | tf_op jit(solution)/shard_map/cond/branch_11_fun/pallas_call | solution.py:93
  142.3 4.1 collective-permute-start.168
  149.0 58.6 %collective-permute-done.164.other_ref = bf16[1536,512]{1,0:T(8,128)(2,1)} collective-permute-done((bf16[1536,512]{1,0:T(8,128)(2,1)}, bf16[1536,512]{1,0:T(8,128)(2,1)}, u32[]{:S(2)}, u32[]{:S(2)}) %collective-permute-start.164) | collective-permute-done | bytes 1572896 | tf_op jit(solution)/shard_map/cond/branch_11_fun/ppermute | solution.py:30
  207.6 5.7 %branch_11_fun.22.own_ref = bf16[1536,512]{1,0:T(8,128)(2,1)} custom-call(bf16[8192,512]{1,0:T(8,128)(2,1)} %get-tuple-element.281.own_ref, bf16[1536,512]{1,0:T(8,128)(2,1)} %collective-permute-done.164.other_ref, bf16[2,1024,512]{2,1,0:T(8,128)(2,1)S(1)} %copy-done.13), custom_call_target="tpu_custom_call" | custom-call | flops 1610612736 | bytes 5767168 | tf_op jit(solution)/shard_map/cond/branch_11_fun/pallas_call | solution.py:93
  213.4 2.7 slice.191
  218.0 99.6 %collective-permute-done.161.lower_ref = bf16[2,4,8192]{2,1,0:T(4,128)(2,1)S(1)} collective-permute-done((bf16[2,4,8192]{2,1,0:T(4,128)(2,1)S(1)}, bf16[2,4,8192]{2,1,0:T(4,128)(2,1)S(1)}, u32[]{:S(2)}, u32[]{:S(2)}) %collective-permute-start.161) | collective-permute-done | bytes 131104 | tf_op jit(solution)/shard_map/cond/branch_11_fun/ppermute | solution.py:30
  318.3 9.1 %branch_11_fun.19.upper_ref = bf16[4,4,8192]{2,1,0:T(4,128)(2,1)} custom-call(bf16[2,4,8192]{2,1,0:T(4,128)(2,1)} %branch_11_fun.18.upper_ref, bf16[2,4,8192]{2,1,0:T(4,128)(2,1)} %copy-done.109), custom_call_target="tpu_custom_call" | custom-call | bytes 524288 | tf_op jit(solution)/shard_map/cond/branch_11_fun/pallas_call | solution.py:164
  327.4 7.0 %branch_11_fun.24.rest_0_ = bf16[8192,512]{1,0:T(8,128)(2,1)} custom-call(bf16[2048,512]{1,0:T(8,128)(2,1)} %branch_11_fun.23.own_ref, bf16[2048,512]{1,0:T(8,128)(2,1)} %collective-permute-done.168.other_ref, bf16[2,1024,512]{2,1,0:T(8,128)(2,1)S(1)} %copy-done.13), custom_call_target="tpu_custom_call" | custom-call | flops 2147483648 | bytes 7340032 | tf_op jit(solution)/shard_map/cond/branch_11_fun/pallas_call | solution.py:93
  334.4 5.6 %branch_11_fun.25.own_ref = bf16[1536,512]{1,0:T(8,128)(2,1)} custom-call(bf16[8192,512]{1,0:T(8,128)(2,1)} %get-tuple-element.281.own_ref, bf16[1536,512]{1,0:T(8,128)(2,1)} %collective-permute-done.167.other_ref, bf16[2,1024,512]{2,1,0:T(8,128)(2,1)S(1)} %copy-done.13), custom_call_target="tpu_custom_call" | custom-call | flops 1610612736 | bytes 5767168 | tf_op jit(solution)/shard_map/cond/branch_11_fun/pallas_call | solution.py:93
  342.6 5.7 %branch_11_fun.26.rest_0_ = bf16[8192,512]{1,0:T(8,128)(2,1)} custom-call(bf16[1536,512]{1,0:T(8,128)(2,1)} %branch_11_fun.22.own_ref, bf16[1536,512]{1,0:T(8,128)(2,1)} %collective-permute-done.169.other_ref, bf16[2,1024,512]{2,1,0:T(8,128)(2,1)S(1)} %copy-done.13, bf16[8192,512]{1,0:T(8,128)(2,1)} %branch_11_fun.24.rest_0_), custom_call_target="tpu_custom_call", output_to_operand_aliasing={{}: (3, {})} | custom-call | flops 1610612736 | bytes 5767168 | tf_op jit(solution)/shard_map/cond/branch_11_fun/pallas_call | solution.py:93
  350.7 3.0 collective-permute-start.171
  353.6 5.6 %branch_11_fun.27.own_ref = bf16[1536,512]{1,0:T(8,128)(2,1)} custom-call(bf16[8192,512]{1,0:T(8,128)(2,1)} %get-tuple-element.281.own_ref, bf16[1536,512]{1,0:T(8,128)(2,1)} %collective-permute-done.165.other_ref, bf16[2,1024,512]{2,1,0:T(8,128)(2,1)S(1)} %copy-done.13), custom_call_target="tpu_custom_call" | custom-call | flops 1610612736 | bytes 5767168 | tf_op jit(solution)/shard_map/cond/branch_11_fun/pallas_call | solution.py:93
  362.9 5.3 %collective-permute-done.162.lower_ref = bf16[4,4,8192]{2,1,0:T(4,128)(2,1)S(1)} collective-permute-done((bf16[4,4,8192]{2,1,0:T(4,128)(2,1)S(1)}, bf16[4,4,8192]{2,1,0:T(4,128)(2,1)S(1)}, u32[]{:S(2)}, u32[]{:S(2)}) %collective-permute-start.162) | collective-permute-done | bytes 262176 | tf_op jit(solution)/shard_map/cond/branch_11_fun/ppermute | solution.py:30
  369.0 17.0 %branch_11_fun.20.upper_ref = bf16[8,4,8192]{2,1,0:T(4,128)(2,1)} custom-call(bf16[4,4,8192]{2,1,0:T(4,128)(2,1)} %branch_11_fun.19.upper_ref, bf16[4,4,8192]{2,1,0:T(4,128)(2,1)} %copy-done.97), custom_call_target="tpu_custom_call" | custom-call | bytes 1048576 | tf_op jit(solution)/shard_map/cond/branch_11_fun/pallas_call | solution.py:164
  386.0 14.7 %collective-permute-done.172.other_ref = bf16[1536,512]{1,0:T(8,128)(2,1)} collective-permute-done((bf16[1536,512]{1,0:T(8,128)(2,1)}, bf16[1536,512]{1,0:T(8,128)(2,1)}, u32[]{:S(2)}, u32[]{:S(2)}) %collective-permute-start.172) | collective-permute-done | bytes 1572896 | tf_op jit(solution)/shard_map/cond/branch_11_fun/ppermute | solution.py:30
  400.7 5.7 %branch_11_fun.28.rest_0_ = bf16[8192,512]{1,0:T(8,128)(2,1)} custom-call(bf16[1536,512]{1,0:T(8,128)(2,1)} %branch_11_fun.25.own_ref, bf16[1536,512]{1,0:T(8,128)(2,1)} %collective-permute-done.172.other_ref, bf16[2,1024,512]{2,1,0:T(8,128)(2,1)S(1)} %copy-done.13, bf16[8192,512]{1,0:T(8,128)(2,1)} %branch_11_fun.26.rest_0_), custom_call_target="tpu_custom_call", output_to_operand_aliasing={{}: (3, {})} | custom-call | flops 1610612736 | bytes 5767168 | tf_op jit(solution)/shard_map/cond/branch_11_fun/pallas_call | solution.py:93
  407.4 4.3 branch_11_fun.29.own_ref
  413.7 4.9 collective-permute-start.170
  418.7 27.0 %collective-permute-done.173.other_ref = bf16[1536,512]{1,0:T(8,128)(2,1)} collective-permute-done((bf16[1536,512]{1,0:T(8,128)(2,1)}, bf16[1536,512]{1,0:T(8,128)(2,1)}, u32[]{:S(2)}, u32[]{:S(2)}) %collective-permute-start.173) | collective-permute-done | bytes 1572896 | tf_op jit(solution)/shard_map/cond/branch_11_fun/ppermute | solution.py:30
  445.6 5.7 %branch_11_fun.30.rest_0_ = bf16[8192,512]{1,0:T(8,128)(2,1)} custom-call(bf16[1536,512]{1,0:T(8,128)(2,1)} %branch_11_fun.27.own_ref, bf16[1536,512]{1,0:T(8,128)(2,1)} %collective-permute-done.173.other_ref, bf16[2,1024,512]{2,1,0:T(8,128)(2,1)S(1)} %copy-done.13, bf16[8192,512]{1,0:T(8,128)(2,1)} %branch_11_fun.28.rest_0_), custom_call_target="tpu_custom_call", output_to_operand_aliasing={{}: (3, {})} | custom-call | flops 1610612736 | bytes 5767168 | tf_op jit(solution)/shard_map/cond/branch_11_fun/pallas_call | solution.py:93
  451.3 13.9 %collective-permute-done.170.other_ref = bf16[512,512]{1,0:T(8,128)(2,1)} collective-permute-done((bf16[512,512]{1,0:T(8,128)(2,1)}, bf16[512,512]{1,0:T(8,128)(2,1)}, u32[]{:S(2)}, u32[]{:S(2)}) %collective-permute-start.170) | collective-permute-done | bytes 524320 | tf_op jit(solution)/shard_map/cond/branch_11_fun/ppermute | solution.py:30
  465.2 3.0 branch_11_fun.31.own_ref
  468.2 6.4 %collective-permute-start.175 = (bf16[512,512]{1,0:T(8,128)(2,1)}, bf16[512,512]{1,0:T(8,128)(2,1)}, u32[]{:S(2)}, u32[]{:S(2)}) collective-permute-start(bf16[512,512]{1,0:T(8,128)(2,1)} %branch_11_fun.31.own_ref), channel_id=1, source_target_pairs={{0,4},{1,5},{2,6},{3,7},{4,0},{5,1},{6,2},{7,3},{8,12},{9,13},{10,... | collective-permute-start | bytes 1572872 | tf_op jit(solution)/shard_map/cond/branch_11_fun/ppermute | solution.py:30
  474.6 32.9 %branch_11_fun.21 = bf16[16,4,8192]{2,1,0:T(4,128)(2,1)} custom-call(bf16[8,4,8192]{2,1,0:T(4,128)(2,1)} %branch_11_fun.20.upper_ref, bf16[8,4,8192]{2,1,0:T(4,128)(2,1)} %collective-permute-done.163.lower_ref), custom_call_target="tpu_custom_call" | custom-call | bytes 2097152 | tf_op jit(solution)/shard_map/cond/branch_11_fun/pallas_call | solution.py:164
  510.7 4.3 branch_11_fun.32.basis_ref.rest_0_
  515.1 11.1 %branch_11_fun.33.rest_0_ = f32[64,512]{1,0:T(8,128)} custom-call(bf16[64,8192]{1,0:T(8,128)(2,1)} %reshape.91.samples_ref, bf16[8192,512]{1,0:T(8,128)(2,1)} %branch_11_fun.32.basis_ref.rest_0_), custom_call_target="tpu_custom_call" | custom-call | flops 503316480 | bytes 8912896 | tf_op jit(solution)/shard_map/cond/branch_11_fun/pallas_call | solution.py:129
  526.2 3.0 branch_11_fun.34.basis_ref
  (61 shorter events, 30.9 us)
Async XLA Ops:
  0.6 0.9 copy-start
  32.6 102.6 %copy-start.13 = (bf16[2,1024,512]{2,1,0:T(8,128)(2,1)S(1)}, bf16[2,1024,512]{2,1,0:T(8,128)(2,1)}, u32[]{:S(2)}) copy-start(bf16[2,1024,512]{2,1,0:T(8,128)(2,1)} %get-tuple-element.271.maps_ref) | copy-start | bytes 6291460 | tf_op jit(solution)/shard_map/cond
  32.6 102.6 %collective-permute-start.166 = (bf16[2048,512]{1,0:T(8,128)(2,1)}, bf16[2048,512]{1,0:T(8,128)(2,1)}, u32[]{:S(2)}, u32[]{:S(2)}) collective-permute-start(bf16[2048,512]{1,0:T(8,128)(2,1)} %slice.213), channel_id=1, source_target_pairs={{0,8},{1,9},{2,10},{3,11},{4,12},{5,13},{6,14},{7,15},{8,0},{9,1},... | collective-permute-start | bytes 6291464 | tf_op jit(solution)/shard_map/cond/branch_11_fun/ppermute | solution.py:30
  35.2 93.6 %collective-permute-start.160 = (bf16[1,4,8192]{2,1,0:T(4,128)(2,1)S(1)}, bf16[1,4,8192]{2,1,0:T(4,128)(2,1)S(1)}, u32[]{:S(2)}, u32[]{:S(2)}) collective-permute-start(bf16[1,4,8192]{2,1,0:T(4,128)(2,1)S(1)} %bitcast.40), channel_id=1, source_target_pairs={{0,8},{1,9},{2,10},{3,11},{4,12},{5,13},{6,14},{7,15},{8,0},{9,1},... | collective-permute-start | bytes 196616 | tf_op jit(solution)/shard_map/cond/branch_11_fun/ppermute | solution.py:30
  128.9 0.6 copy-start.121
  135.3 72.3 %collective-permute-start.164 = (bf16[1536,512]{1,0:T(8,128)(2,1)}, bf16[1536,512]{1,0:T(8,128)(2,1)}, u32[]{:S(2)}, u32[]{:S(2)}) collective-permute-start(bf16[1536,512]{1,0:T(8,128)(2,1)} %slice.190), channel_id=1, source_target_pairs={{0,8},{1,9},{2,10},{3,11},{4,12},{5,13},{6,14},{7,15},{8,0},{9,1},... | collective-permute-start | bytes 4718600 | tf_op jit(solution)/shard_map/cond/branch_11_fun/ppermute | solution.py:30
  142.3 185.1 %collective-permute-start.168 = (bf16[2048,512]{1,0:T(8,128)(2,1)}, bf16[2048,512]{1,0:T(8,128)(2,1)}, u32[]{:S(2)}, u32[]{:S(2)}) collective-permute-start(bf16[2048,512]{1,0:T(8,128)(2,1)} %branch_11_fun.23.own_ref), channel_id=1, source_target_pairs={{0,4},{1,5},{2,6},{3,7},{4,0},{5,1},{6,2},{7,3},{8,12},{9,13},{10,... | collective-permute-start | bytes 6291464 | tf_op jit(solution)/shard_map/cond/branch_11_fun/ppermute | solution.py:30
  149.0 185.4 %collective-permute-start.167 = (bf16[1536,512]{1,0:T(8,128)(2,1)}, bf16[1536,512]{1,0:T(8,128)(2,1)}, u32[]{:S(2)}, u32[]{:S(2)}) collective-permute-start(bf16[1536,512]{1,0:T(8,128)(2,1)} %slice.193), channel_id=1, source_target_pairs={{0,8},{1,9},{2,10},{3,11},{4,12},{5,13},{6,14},{7,15},{8,0},{9,1},... | collective-permute-start | bytes 4718600 | tf_op jit(solution)/shard_map/cond/branch_11_fun/ppermute | solution.py:30
  213.3 2.8 copy-start.77
  213.3 129.3 %collective-permute-start.169 = (bf16[1536,512]{1,0:T(8,128)(2,1)}, bf16[1536,512]{1,0:T(8,128)(2,1)}, u32[]{:S(2)}, u32[]{:S(2)}) collective-permute-start(bf16[1536,512]{1,0:T(8,128)(2,1)} %branch_11_fun.22.own_ref), channel_id=1, source_target_pairs={{0,4},{1,5},{2,6},{3,7},{4,0},{5,1},{6,2},{7,3},{8,12},{9,13},{10,... | collective-permute-start | bytes 4718600 | tf_op jit(solution)/shard_map/cond/branch_11_fun/ppermute | solution.py:30
  216.0 132.3 %collective-permute-start.165 = (bf16[1536,512]{1,0:T(8,128)(2,1)}, bf16[1536,512]{1,0:T(8,128)(2,1)}, u32[]{:S(2)}, u32[]{:S(2)}) collective-permute-start(bf16[1536,512]{1,0:T(8,128)(2,1)} %slice.191), channel_id=1, source_target_pairs={{0,8},{1,9},{2,10},{3,11},{4,12},{5,13},{6,14},{7,15},{8,0},{9,1},... | collective-permute-start | bytes 4718600 | tf_op jit(solution)/shard_map/cond/branch_11_fun/ppermute | solution.py:30
  216.0 101.6 %collective-permute-start.161 = (bf16[2,4,8192]{2,1,0:T(4,128)(2,1)S(1)}, bf16[2,4,8192]{2,1,0:T(4,128)(2,1)S(1)}, u32[]{:S(2)}, u32[]{:S(2)}) collective-permute-start(bf16[2,4,8192]{2,1,0:T(4,128)(2,1)S(1)} %copy-done.77), channel_id=1, source_target_pairs={{0,4},{1,5},{2,6},{3,7},{4,0},{5,1},{6,2},{7,3},{8,12},{9,13},{10,... | collective-permute-start | bytes 393224 | tf_op jit(solution)/shard_map/cond/branch_11_fun/ppermute | solution.py:30
  317.7 0.7 copy-start.109
  340.1 60.7 %collective-permute-start.172 = (bf16[1536,512]{1,0:T(8,128)(2,1)}, bf16[1536,512]{1,0:T(8,128)(2,1)}, u32[]{:S(2)}, u32[]{:S(2)}) collective-permute-start(bf16[1536,512]{1,0:T(8,128)(2,1)} %branch_11_fun.25.own_ref), channel_id=1, source_target_pairs={{0,4},{1,5},{2,6},{3,7},{4,0},{5,1},{6,2},{7,3},{8,12},{9,13},{10,... | collective-permute-start | bytes 4718600 | tf_op jit(solution)/shard_map/cond/branch_11_fun/ppermute | solution.py:30
  350.7 10.7 %copy-start.63 = (bf16[4,4,8192]{2,1,0:T(4,128)(2,1)S(1)}, bf16[4,4,8192]{2,1,0:T(4,128)(2,1)}, u32[]{:S(2)}) copy-start(bf16[4,4,8192]{2,1,0:T(4,128)(2,1)} %branch_11_fun.19.upper_ref) | copy-start | bytes 786436 | tf_op jit(solution)/shard_map/cond
  350.7 55.7 %collective-permute-start.171 = (bf16[1024,512]{1,0:T(8,128)(2,1)}, bf16[1024,512]{1,0:T(8,128)(2,1)S(1)}, u32[]{:S(2)}, u32[]{:S(2)}) collective-permute-start(bf16[1024,512]{1,0:T(8,128)(2,1)} %slice.195), channel_id=1, source_target_pairs={{0,8},{1,9},{2,10},{3,11},{4,12},{5,13},{6,14},{7,15},{8,0},{9,1},... | collective-permute-start | bytes 3145736 | tf_op jit(solution)/shard_map/cond/branch_11_fun/ppermute | solution.py:30
  359.3 86.3 %collective-permute-start.173 = (bf16[1536,512]{1,0:T(8,128)(2,1)}, bf16[1536,512]{1,0:T(8,128)(2,1)}, u32[]{:S(2)}, u32[]{:S(2)}) collective-permute-start(bf16[1536,512]{1,0:T(8,128)(2,1)} %branch_11_fun.27.own_ref), channel_id=1, source_target_pairs={{0,4},{1,5},{2,6},{3,7},{4,0},{5,1},{6,2},{7,3},{8,12},{9,13},{10,... | collective-permute-start | bytes 4718600 | tf_op jit(solution)/shard_map/cond/branch_11_fun/ppermute | solution.py:30
  361.4 6.9 %collective-permute-start.162 = (bf16[4,4,8192]{2,1,0:T(4,128)(2,1)S(1)}, bf16[4,4,8192]{2,1,0:T(4,128)(2,1)S(1)}, u32[]{:S(2)}, u32[]{:S(2)}) collective-permute-start(bf16[4,4,8192]{2,1,0:T(4,128)(2,1)S(1)} %copy-done.63), channel_id=1, source_target_pairs={{0,2},{1,3},{2,0},{3,1},{4,6},{5,7},{6,4},{7,5},{8,10},{9,11},{10,... | collective-permute-start | bytes 786440 | tf_op jit(solution)/shard_map/cond/branch_11_fun/ppermute | solution.py:30
  368.2 0.7 copy-start.97
  406.4 12.3 %copy-start.24 = (bf16[8,4,8192]{2,1,0:T(4,128)(2,1)S(1)}, bf16[8,4,8192]{2,1,0:T(4,128)(2,1)}, u32[]{:S(2)}) copy-start(bf16[8,4,8192]{2,1,0:T(4,128)(2,1)} %branch_11_fun.20.upper_ref) | copy-start | bytes 1572868 | tf_op jit(solution)/shard_map/cond
  406.4 1.0 copy-start.44
  411.7 98.0 %collective-permute-start.174 = (bf16[1024,512]{1,0:T(8,128)(2,1)}, bf16[1024,512]{1,0:T(8,128)(2,1)S(1)}, u32[]{:S(2)}, u32[]{:S(2)}) collective-permute-start(bf16[1024,512]{1,0:T(8,128)(2,1)} %branch_11_fun.29.own_ref), channel_id=1, source_target_pairs={{0,4},{1,5},{2,6},{3,7},{4,0},{5,1},{6,2},{7,3},{8,12},{9,13},{10,... | collective-permute-start | bytes 3145736 | tf_op jit(solution)/shard_map/cond/branch_11_fun/ppermute | solution.py:30
  413.7 51.5 %collective-permute-start.170 = (bf16[512,512]{1,0:T(8,128)(2,1)}, bf16[512,512]{1,0:T(8,128)(2,1)}, u32[]{:S(2)}, u32[]{:S(2)}) collective-permute-start(bf16[512,512]{1,0:T(8,128)(2,1)} %slice.194), channel_id=1, source_target_pairs={{0,8},{1,9},{2,10},{3,11},{4,12},{5,13},{6,14},{7,15},{8,0},{9,1},... | collective-permute-start | bytes 1572872 | tf_op jit(solution)/shard_map/cond/branch_11_fun/ppermute | solution.py:30
  418.7 56.0 %collective-permute-start.163 = (bf16[8,4,8192]{2,1,0:T(4,128)(2,1)S(1)}, bf16[8,4,8192]{2,1,0:T(4,128)(2,1)}, u32[]{:S(2)}, u32[]{:S(2)}) collective-permute-start(bf16[8,4,8192]{2,1,0:T(4,128)(2,1)S(1)} %copy-done.24), channel_id=1, source_target_pairs={{0,1},{1,0},{2,3},{3,2},{4,5},{5,4},{6,7},{7,6},{8,9},{9,8},{10,11... | collective-permute-start | bytes 1572872 | tf_op jit(solution)/shard_map/cond/branch_11_fun/ppermute | solution.py:30
  468.2 57.9 %collective-permute-start.175 = (bf16[512,512]{1,0:T(8,128)(2,1)}, bf16[512,512]{1,0:T(8,128)(2,1)}, u32[]{:S(2)}, u32[]{:S(2)}) collective-permute-start(bf16[512,512]{1,0:T(8,128)(2,1)} %branch_11_fun.31.own_ref), channel_id=1, source_target_pairs={{0,4},{1,5},{2,6},{3,7},{4,0},{5,1},{6,2},{7,3},{8,12},{9,13},{10,... | collective-permute-start | bytes 1572872 | tf_op jit(solution)/shard_map/cond/branch_11_fun/ppermute | solution.py:30
  509.7 1.0 copy-start.36
  530.8 2.3 copy-start.1
